TPU v7x, 256 devices: a whole 4x4x8 slice. The times are simulated.
256 devices in a mesh: hid: 32 (over z, y), wid: 8 (over x, core).
Axes of the slice: x: 4, y: 4, z: 8, core: 2. Of those that a mesh axis runs over, the one named last changes fastest.
Arguments:
- inputs: bfloat16 [256, 12288], P(None, 'wid'), may hold values from -6 to 6
- gate_pre: bfloat16 [256, 32768], P(None, 'hid'), may hold values from -8 to 8
- up_pre: bfloat16 [256, 32768], P(None, 'hid'), may hold values from -6 to 6
- out_grad: bfloat16 [256, 12288], P(None, 'wid'), may hold values from -6 to 6
- gate_codes: int32 [6144, 32768], P('wid', 'hid'), may hold values from 0 to 255
- up_codes: int32 [6144, 32768], P('wid', 'hid'), may hold values from 0 to 255
- down_codes: int32 [16384, 12288], P('hid', 'wid'), may hold values from 0 to 255
- gate_scale: float32 [96, 32768], P('wid', 'hid'), may hold values from 0.0010825318 to 0.0027063293
- up_scale: float32 [96, 32768], P('wid', 'hid'), may hold values from 0.0010825318 to 0.0027063293
- down_scale: float32 [256, 12288], P('hid', 'wid'), may hold values from 0.0006629126 to 0.0016572815
Outputs:
- input_grad: bfloat16 [256, 12288], P('hid', 'wid')
- gate_log_grad: float32 [96, 32768], P('wid', 'hid')
- up_log_grad: float32 [96, 32768], P('wid', 'hid')
- down_log_grad: float32 [256, 12288], P('hid', 'wid')
Inputs may be any that keep to these rules, and one draw needn't show every extreme that they name: `gate_codes`: each word holds two independent four-bit codes. `up_codes`: each word holds two independent four-bit codes. `down_codes`: each word holds two independent four-bit codes.
All inputs are finite; a program needn't handle non-finite values.
Results may differ from a plain program's by a relative error of at most 0.007.
Values may be sent and summed in bfloat16 or wider, within the bound.
A program may use at most 128 MiB of HBM per device.

v0:
```python
import jax
import jax.numpy as jnp
from jax import lax
from jax.sharding import PartitionSpec as P

HB = 4096
GROUP = 128


def from_partner(value, axis, bit):
    mask = 2**bit
    pairs = [(source, source ^ mask) for source in range(lax.axis_size(axis))]
    return lax.ppermute(value, axis, pairs)


def unpack_centred(packed):
    shifts = 4 * jnp.arange(2, dtype=jnp.int32)
    nibbles = jnp.bitwise_and(jnp.right_shift(packed[:, None, :], shifts[None, :, None]), 15)
    nibbles = nibbles.reshape(packed.shape[0] * 2, packed.shape[1])
    return (nibbles - 8).astype(jnp.float32)


def dequantize(packed, scales):
    centred = unpack_centred(packed)
    weight = (centred * jnp.repeat(scales, GROUP, axis=0)).astype(jnp.bfloat16)
    return (weight, centred)


def signs_table(extent):
    indices = jnp.arange(extent, dtype=jnp.int32)
    common_bits = jnp.bitwise_and(indices[:, None], indices[None, :])
    parity = jnp.zeros((extent, extent), jnp.int32)
    for bit_index in range(extent.bit_length() - 1):
        parity = parity + jnp.bitwise_and(jnp.right_shift(common_bits, bit_index), 1)
    return (1 - 2 * (parity % 2)).astype(jnp.bfloat16)


def group_sum(values, centred, scales):
    height, across = values.shape
    return scales * (centred * values).reshape(height // GROUP, GROUP, across).sum(axis=1)


def shards(
    inputs,
    gate_pre,
    up_pre,
    out_grad,
    gate_codes,
    up_codes,
    down_codes,
    gate_scale,
    up_scale,
    down_scale,
):
    hid_width = gate_pre.shape[1]
    gate_weight, gate_centred = dequantize(gate_codes, gate_scale)
    up_weight, up_centred = dequantize(up_codes, up_scale)
    down_weight, down_centred = dequantize(down_codes, down_scale)
    partial_value = lax.dot_general(
        out_grad, down_weight, (((1,), (1,)), ((), ())), preferred_element_type=jnp.float32
    )
    summed = lax.psum(partial_value, "wid")
    rotated_grad = summed.astype(jnp.bfloat16)
    gate_val = gate_pre.astype(jnp.float32)
    up_val = up_pre.astype(jnp.float32)
    activated = jax.nn.silu(gate_val)
    hidden = (activated * up_val).astype(jnp.bfloat16)
    signs = signs_table(hid_width)
    turn_fwd = jnp.dot(hidden, signs, preferred_element_type=jnp.float32)
    turn_back = jnp.dot(rotated_grad, signs, preferred_element_type=jnp.float32)
    position = lax.axis_index("hid")
    for bit_index in range((HB // hid_width).bit_length() - 1):
        far_fwd, far_back = from_partner((turn_fwd, turn_back), "hid", bit_index)
        upper_half = jnp.bitwise_and(jnp.right_shift(position, bit_index), 1) == 1
        turn_fwd = jnp.where(upper_half, far_fwd - turn_fwd, turn_fwd + far_fwd)
        turn_back = jnp.where(upper_half, far_back - turn_back, turn_back + far_back)
    scaling = HB ** (-0.5)
    rotated = (turn_fwd * scaling).astype(jnp.bfloat16)
    hidden_grad = turn_back * scaling
    sigmoid_gate = jax.nn.sigmoid(gate_val)
    slope = sigmoid_gate * (1.0 + gate_val * (1.0 - sigmoid_gate))
    gate_grad = (hidden_grad * up_val * slope).astype(jnp.bfloat16)
    up_grad = (hidden_grad * activated).astype(jnp.bfloat16)
    contract = (((1,), (1,)), ((), ()))
    first_term = lax.dot_general(
        gate_grad, gate_weight, contract, preferred_element_type=jnp.float32
    )
    grad_inputs = lax.psum_scatter(
        first_term
        + lax.dot_general(up_grad, up_weight, contract, preferred_element_type=jnp.float32),
        "hid",
        scatter_dimension=0,
        tiled=True,
    ).astype(jnp.bfloat16)
    token_contract = (((0,), (0,)), ((), ()))
    gate_full = lax.dot_general(
        inputs, gate_grad, token_contract, preferred_element_type=jnp.float32
    )
    gate_log_grad = group_sum(gate_full, gate_centred, gate_scale)
    up_full = lax.dot_general(inputs, up_grad, token_contract, preferred_element_type=jnp.float32)
    up_log_grad = group_sum(up_full, up_centred, up_scale)
    down_full = lax.dot_general(
        rotated, out_grad, token_contract, preferred_element_type=jnp.float32
    )
    down_log_grad = group_sum(down_full, down_centred, down_scale)
    return (grad_inputs, gate_log_grad, up_log_grad, down_log_grad)


def solution(mesh):
    in_specs = (
        P(None, "wid"),
        P(None, "hid"),
        P(None, "hid"),
        P(None, "wid"),
        P("wid", "hid"),
        P("wid", "hid"),
        P("hid", "wid"),
        P("wid", "hid"),
        P("wid", "hid"),
        P("hid", "wid"),
    )
    out_specs = (P("hid", "wid"), P("wid", "hid"), P("wid", "hid"), P("hid", "wid"))
    return jax.shard_map(shards, mesh=mesh, in_specs=in_specs, out_specs=out_specs, check_vma=False)
```

profile of v0, /device:TPU:1, one launch (start us, length us, event | category | flops | bytes accessed | tf_op | source)
XLA Modules:
  0.0 422.8 jit_solution(3155021112805887350)
XLA Ops:
  7.4 6.8 %shift_right_arithmetic.142 = s32[512,2,1536]{2,1,0:T(2,128)} broadcast(s32[512,1536]{1,0:T(8,128)} %param.16), dimensions={0,2} | broadcast | bytes 9437184 | tf_op jit(solution)/shard_map/shift_right_arithmetic | solution.py:18
  14.3 8.4 %shift_right_arithmetic.143 = s32[1024,1536]{1,0:T(8,128)} reshape(s32[512,2,1536]{2,1,0:T(2,128)} %shift_right_arithmetic.142) | data formatting | bytes 12582912 | tf_op jit(solution)/shard_map/shift_right_arithmetic | solution.py:18
  22.7 3.6 fusion
  27.3 52.2 %all-reduce.1 = bf16[256,1024]{0,1:T(8,128)(2,1)S(1)} all-reduce(f32[256,1024]{0,1:T(8,128)S(1)} %convolution_bitcast_fusion), channel_id=1, replica_groups=mesh['hid'=32,'wid'=8] {'wid'}, use_global_device_ids=true, to_apply=%region_0.0 | all-reduce | flops 262144 | bytes 1572864 | tf_op jit(solution)/shard_map/psum | solution.py:62
  79.6 6.8 %fusion.16 = f32[256,1024]{1,0:T(8,128)S(1)} fusion(bf16[256,1024]{0,1:T(8,128)(2,1)S(1)} %all-reduce.1), kind=kOutput, calls=%fused_computation.28 | convolution fusion | flops 583008256 | bytes 1572864 | tf_op jit(solution)/shard_map/dot_general | solution.py:70
  86.5 23.1 %collective-permute-done = f32[256,1024]{1,0:T(8,128)} collective-permute-done((f32[256,1024]{1,0:T(8,128)S(1)}, f32[256,1024]{1,0:T(8,128)}, u32[]{:S(2)}, u32[]{:S(2)}) %collective-permute-start) | collective-permute-done | bytes 1048608 | tf_op jit(solution)/shard_map/ppermute | solution.py:13
  111.3 8.7 %fusion.14 = f32[256,1024]{1,0:T(8,128)} fusion(bf16[256,1024]{1,0:T(8,128)(2,1)} %param.12, bf16[256,1024]{1,0:T(8,128)(2,1)S(1)} %copy-done.1), kind=kOutput, calls=%fused_computation.27 | convolution fusion | flops 585105408 | bytes 2097152 | tf_op jit(solution)/shard_map/dot_general | solution.py:69
  120.3 6.7 %shift_right_arithmetic.166 = s32[768,2,1024]{2,1,0:T(2,128)} broadcast(s32[768,1024]{1,0:T(8,128)} %param.14), dimensions={0,2} | broadcast | bytes 9437184 | tf_op jit(solution)/shard_map/shift_right_arithmetic | solution.py:18
  127.0 8.5 %shift_right_arithmetic.167 = s32[1536,1024]{1,0:T(8,128)} reshape(s32[768,2,1024]{2,1,0:T(2,128)} %shift_right_arithmetic.166) | data formatting | bytes 12582912 | tf_op jit(solution)/shard_map/shift_right_arithmetic | solution.py:18
  135.5 6.5 %copy.18 = s32[1536,1024]{0,1:T(8,128)} copy(s32[1536,1024]{1,0:T(8,128)} %shift_right_arithmetic.167) | data formatting | bytes 12582912 | tf_op jit(solution)/shard_map/shift_right_arithmetic | solution.py:18
  142.0 6.7 %shift_right_arithmetic.172 = s32[768,2,1024]{2,1,0:T(2,128)} broadcast(s32[768,1024]{1,0:T(8,128)} %param.15), dimensions={0,2} | broadcast | bytes 9437184 | tf_op jit(solution)/shard_map/shift_right_arithmetic | solution.py:18
  148.7 8.5 %shift_right_arithmetic.173 = s32[1536,1024]{1,0:T(8,128)} reshape(s32[768,2,1024]{2,1,0:T(2,128)} %shift_right_arithmetic.172) | data formatting | bytes 12582912 | tf_op jit(solution)/shard_map/shift_right_arithmetic | solution.py:18
  157.2 6.6 %copy.20 = s32[1536,1024]{0,1:T(8,128)} copy(s32[1536,1024]{1,0:T(8,128)} %shift_right_arithmetic.173) | data formatting | bytes 12582912 | tf_op jit(solution)/shard_map/shift_right_arithmetic | solution.py:18
  163.8 3.5 broadcast_in_dim.7
  167.3 6.6 %copy.19 = f32[1536,1024]{0,1:T(8,128)} copy(f32[1536,1024]{1,0:T(8,128)} %bitcast.34) | data formatting | bytes 12582912 | tf_op jit(solution)/shard_map/reshape | solution.py:25
  173.9 3.5 broadcast_in_dim.8
  177.4 6.6 %copy.21 = f32[1536,1024]{0,1:T(8,128)} copy(f32[1536,1024]{1,0:T(8,128)} %bitcast.35) | data formatting | bytes 12582912 | tf_op jit(solution)/shard_map/reshape | solution.py:25
  184.0 2.2 multiply_convert_fusion.7
  186.3 6.3 %fusion.5 = f32[256,1536]{1,0:T(8,128)S(1)} fusion(bf16[256,1024]{1,0:T(8,128)(2,1)S(1)} %get-tuple-element.5, f32[1536,1024]{0,1:T(8,128)} %copy.19, s32[1536,1024]{0,1:T(8,128)} %copy.18, s32[1536]{0:T(1024)S(1)} %shift_right_arithmetic.169), kind=kOutput, calls=%fused_computation.18 | convolution fusion | flops 814743552 | bytes 14686208 | tf_op jit(solution)/shard_map/dot_general | solution.py:85
  193.3 2.8 fusion.13
  196.2 1.9 add_select_fusion.1
  198.1 3.3 collective-permute-start.3
  201.4 19.3 %collective-permute-done.3 = f32[256,1024]{1,0:T(8,128)S(1)} collective-permute-done((f32[256,1024]{1,0:T(8,128)S(1)}, f32[256,1024]{1,0:T(8,128)S(1)}, u32[]{:S(2)}, u32[]{:S(2)}) %collective-permute-start.3) | collective-permute-done | bytes 1048608 | tf_op jit(solution)/shard_map/ppermute | solution.py:13
  220.7 4.1 bitcast_reduce_fusion
  225.5 3.8 bitcast_multiply_fusion
  229.3 6.6 %copy.23 = f32[1536,1024]{1,0:T(8,128)} copy(f32[1536,1024]{0,1:T(8,128)} %bitcast_multiply_fusion) | data formatting | bytes 12582912 | tf_op jit(solution)/shard_map/mul | solution.py:40
  235.9 3.5 reduce_sum.28
  240.0 6.6 %bitcast_multiply_fusion.1 = f32[1536,1024]{0,1:T(8,128)} fusion(s32[1536,1024]{0,1:T(8,128)} %copy.18, bf16[256,1024]{1,0:T(8,128)(2,1)S(1)} %get-tuple-element.5, bf16[256,1536]{1,0:T(8,128)(2,1)S(1)} %copy-done, s32[1536]{0:T(1024)S(1)} %shift_right_arithmetic.169), kind=kOutput, calls=%fused_computation.2 | convolution fusion | flops 813170688 | bytes 13899776 | tf_op jit(solution)/shard_map/dot_general | solution.py:96
  246.7 6.6 %copy.22 = f32[1536,1024]{1,0:T(8,128)} copy(f32[1536,1024]{0,1:T(8,128)} %bitcast_multiply_fusion.1) | data formatting | bytes 12582912 | tf_op jit(solution)/shard_map/mul | solution.py:40
  253.3 3.5 reduce_sum.27
  257.4 157.1 %reduce-scatter.2.cloned.1.call-done = f32[8,1536]{1,0:T(8,128)} async-done(((f32[256,1536]{1,0:T(8,128)}), f32[8,1536]{1,0:T(8,128)}) %reduce-scatter.2.cloned.1.call-update) | async-done | bytes 49168 | tf_op jit(solution)/shard_map/reduce_scatter | solution.py:88
  414.5 1.4 convert_element_type.59
  (46 shorter events, 6.0 us)
Async XLA Ops:
  7.2 218.3 %copy-start = (bf16[256,1536]{1,0:T(8,128)(2,1)S(1)}, bf16[256,1536]{1,0:T(8,128)(2,1)}, u32[]{:S(2)}) copy-start(bf16[256,1536]{1,0:T(8,128)(2,1)} %param.10) | copy-start | bytes 2359300
  7.2 407.3 %reduce-scatter.2.cloned.1.call-start = ((), (), s32[]{:S(2)}) async-start(), calls=%async_computation.1 | async-start | bytes 1622016 | tf_op jit(solution)/shard_map/reduce_scatter | solution.py:88
  14.3 8.4 %copy-start.4 = (f32[8,1536]{1,0:T(8,128)S(1)}, f32[8,1536]{1,0:T(8,128)}, u32[]{:S(2)}) copy-start(f32[8,1536]{1,0:T(8,128)} %param.19) | copy-start | bytes 147460
  22.7 3.6 copy-start.6
  79.6 31.8 %copy-start.1 = (bf16[256,1024]{1,0:T(8,128)(2,1)S(1)}, bf16[256,1024]{1,0:T(8,128)(2,1)}, u32[]{:S(2)}) copy-start(bf16[256,1024]{1,0:T(8,128)(2,1)} %param.11) | copy-start | bytes 1572868
  86.4 23.2 %collective-permute-start = (f32[256,1024]{1,0:T(8,128)S(1)}, f32[256,1024]{1,0:T(8,128)}, u32[]{:S(2)}, u32[]{:S(2)}) collective-permute-start(f32[256,1024]{1,0:T(8,128)S(1)} %fusion.16), channel_id=1, source_target_pairs={{0,8},{8,0},{16,24},{24,16},{32,40},{40,32},{48,56},{56,48},{64,72... | collective-permute-start | bytes 3145736 | tf_op jit(solution)/shard_map/ppermute | solution.py:13
  111.0 73.0 %collective-permute-start.1 = (f32[256,1024]{1,0:T(8,128)S(1)}, f32[256,1024]{1,0:T(8,128)}, u32[]{:S(2)}, u32[]{:S(2)}) collective-permute-start(f32[256,1024]{1,0:T(8,128)S(1)} %add_select_fusion.2), channel_id=1, source_target_pairs={{0,16},{8,24},{16,0},{24,8},{32,48},{40,56},{48,32},{56,40},{64,80... | collective-permute-start | bytes 3145736 | tf_op jit(solution)/shard_map/ppermute | solution.py:13
  120.0 76.1 %collective-permute-start.2 = (f32[256,1024]{1,0:T(8,128)}, f32[256,1024]{1,0:T(8,128)}, u32[]{:S(2)}, u32[]{:S(2)}) collective-permute-start(f32[256,1024]{1,0:T(8,128)} %fusion.14), channel_id=1, source_target_pairs={{0,8},{8,0},{16,24},{24,16},{32,40},{40,32},{48,56},{56,48},{64,72... | collective-permute-start | bytes 3145736 | tf_op jit(solution)/shard_map/ppermute | solution.py:13
  157.2 6.6 %copy-start.3 = (f32[12,1024]{1,0:T(8,128)S(1)}, f32[12,1024]{1,0:T(8,128)}, u32[]{:S(2)}) copy-start(f32[12,1024]{1,0:T(8,128)} %param.17) | copy-start | bytes 147460
  167.3 6.6 %copy-start.2 = (f32[12,1024]{1,0:T(8,128)S(1)}, f32[12,1024]{1,0:T(8,128)}, u32[]{:S(2)}) copy-start(f32[12,1024]{1,0:T(8,128)} %param.18) | copy-start | bytes 147460
  184.0 8.5 %slice-start.4 = ((s8[6291456]{0:T(1024)(128)(4,1)}), s8[4194304]{0:T(1024)(128)(4,1)S(1)}, s32[]{:S(2)}) async-start(s8[6291456]{0:T(1024)(128)(4,1)} %bitcast.30), calls=%async_computation.6 | async-start | bytes 8388608
  186.2 6.3 %slice-start = ((s8[6291456]{0:T(1024)(128)(4,1)}), s8[4194304]{0:T(1024)(128)(4,1)S(1)}, s32[]{:S(2)}) async-start(s8[6291456]{0:T(1024)(128)(4,1)} %bitcast.26), calls=%async_computation.2 | async-start | bytes 8388608
  186.2 6.5 %slice-start.1 = ((s8[6291456]{0:T(1024)(128)(4,1)}), s8[2097152]{0:T(1024)(128)(4,1)S(1)}, s32[]{:S(2)}) async-start(s8[6291456]{0:T(1024)(128)(4,1)} %bitcast.26), calls=%async_computation.3 | async-start | bytes 4194304
  186.2 7.1 %slice-start.5 = ((s8[6291456]{0:T(1024)(128)(4,1)}), s8[2097152]{0:T(1024)(128)(4,1)S(1)}, s32[]{:S(2)}) async-start(s8[6291456]{0:T(1024)(128)(4,1)} %bitcast.30), calls=%async_computation.7 | async-start | bytes 4194304
  196.2 29.3 %slice-start.2 = ((s8[6291456]{0:T(1024)(128)(4,1)}), s8[4194304]{0:T(1024)(128)(4,1)S(1)}, s32[]{:S(2)}) async-start(s8[6291456]{0:T(1024)(128)(4,1)} %bitcast.28), calls=%async_computation.4 | async-start | bytes 8388608
  198.1 26.8 %copy-start.5 = (f32[8,1536]{1,0:T(8,128)S(1)}, f32[8,1536]{1,0:T(8,128)}, u32[]{:S(2)}) copy-start(f32[8,1536]{1,0:T(8,128)} %param.19) | copy-start | bytes 147460
  198.1 27.4 %slice-start.3 = ((s8[6291456]{0:T(1024)(128)(4,1)}), s8[2097152]{0:T(1024)(128)(4,1)S(1)}, s32[]{:S(2)}) async-start(s8[6291456]{0:T(1024)(128)(4,1)} %bitcast.28), calls=%async_computation.5 | async-start | bytes 4194304
  198.1 22.6 %collective-permute-start.3 = (f32[256,1024]{1,0:T(8,128)S(1)}, f32[256,1024]{1,0:T(8,128)S(1)}, u32[]{:S(2)}, u32[]{:S(2)}) collective-permute-start(f32[256,1024]{1,0:T(8,128)S(1)} %add_select_fusion.1), channel_id=1, source_target_pairs={{0,16},{8,24},{16,0},{24,8},{32,48},{40,56},{48,32},{56,40},{64,80... | collective-permute-start | bytes 3145736 | tf_op jit(solution)/shard_map/ppermute | solution.py:13
Sparse Core Ops, SparseCore 0:
  196.3 218.2 reduce-scatter.1
where the time goes:
time: 429 us; the launch traced here: 423 us
  waiting for transfers between devices  200 us (47%)
  local copies, waits for them, and re-layouts  93.4 us (22%)
  blocking collectives  52.2 us (12%)
  matrix products  40.2 us (9%)
  other arithmetic  19.4 us (5%)
  between operations  14.3 us (3%)
    reduce_scatter x1, waiting for transfers between devices, shards(): lax.psum_scatter(first_term + lax.dot_general(up_grad, up_weight, contrac...  157 us
    shift_right_arithmetic x12, local copies, waits for them, and re-layouts, unpack_centred(): jnp.right_shift(packed[:, None, :], shifts[None, :, None])  59.2 us
    psum x1, blocking collectives, shards(): summed = lax.psum(partial_value, 'wid')  52.2 us
    ppermute x4, waiting for transfers between devices, from_partner(): return lax.ppermute(value, axis, pairs)  42.4 us
    reshape x2, local copies, waits for them, and re-layouts, dequantize(): weight = (centred * jnp.repeat(scales, GROUP, axis=0)).astype(jnp.bfloat16)  13.2 us
    mul x2, local copies, waits for them, and re-layouts, group_sum(): centred * values  13.2 us
    dot_general x1, matrix products, shards(): turn_fwd = jnp.dot(hidden, signs, preferred_element_type=jnp.float32)  8.72 us
  transfers between devices with their start and end apart: 5, of which 3 were waited for; matrix products, arithmetic and copies ran while one was open for 29% of the time, Pallas kernels for 0%

commit v1 on v0

v1 whole, which is shorter than its diff:
```python
import functools
import jax
import jax.numpy as jnp
from jax import lax
from jax.experimental import pallas as pl
from jax.experimental.pallas import tpu as pltpu
from jax.sharding import PartitionSpec as P

HB = 4096
GROUP = 128
SUB = 256
WORDS = SUB // 2
HALF = GROUP // 2
F32 = jnp.float32
BF16 = jnp.bfloat16
NT = (((1,), (1,)), ((), ()))


def parity(v):
    v = jnp.bitwise_xor(v, jnp.right_shift(v, 4))
    v = jnp.bitwise_xor(v, jnp.right_shift(v, 2))
    v = jnp.bitwise_xor(v, jnp.right_shift(v, 1))
    return jnp.bitwise_and(v, 1)


def natural(k):
    return 2 * jnp.bitwise_and(k, WORDS - 1) + jnp.right_shift(k, 7)


def centred_pair(words):
    low = (jnp.bitwise_and(words, 15) - 8).astype(F32)
    high = (jnp.right_shift(words, 4) - 8).astype(F32)
    return low, high


def body(
    dims,
    inp_hbm, gp_hbm, up_hbm, og_hbm, gc_hbm, uc_hbm, dc_hbm, gs_hbm, us_hbm, ds_hbm,
    gi_out, gl_out, ul_out, dl_out,
    inp, gp, up, og, gc, uc, dc, gs, us, ds,
    gw, uw, dw, act, slope, xt, rt, gg, ug,
    hnat, hperm, pick, unpick,
    pbuf, prx, sbuf, xrx, rg, hd, hga, rta, ybuf, yrx, zbuf, zrx,
    load_sem, dc_sem, gc_sem, uc_sem,
    p_s, p_r, x_s, x_r, y_s, y_r, f_s, f_r, ga_s, ga_r, gp_s, gp_r, ra_s, ra_r, rp_s, rp_r,
    ry_s, ry_r, rz_s, rz_r,
):
    NX, NY, NZ, T, D, F = dims
    NB = F // SUB
    NM = D // SUB
    NC = NM // 2
    TS = T // (2 * NX)
    TH = T // 2
    h = lax.axis_index("hid")
    w = lax.axis_index("wid")
    x = w // 2
    core = w % 2
    z = h // NY
    y = h % NY
    mine = core * NX + x

    def x_dev(k):
        return (h, lax.rem(x + k, NX) * 2 + core)

    def y_dev(k):
        return (z * NY + lax.rem(y + k, NY), w)

    def z_dev(k):
        return (lax.rem(z + k, NZ) * NY + y, w)

    partner = (h, x * 2 + 1 - core)

    def remote(src, dst, ssem, rsem, dev):
        return pltpu.make_async_remote_copy(
            src_ref=src, dst_ref=dst, send_sem=ssem, recv_sem=rsem,
            device_id=dev, device_id_type=pl.DeviceIdType.MESH,
        )

    barrier = pltpu.get_barrier_semaphore()
    peers = [partner] + [x_dev(k) for k in range(1, NX)] + [y_dev(k) for k in range(1, NY)]
    peers += [z_dev(k) for k in range(1, NZ)]
    for dev in peers:
        pl.semaphore_signal(barrier, inc=1, device_id=dev, device_id_type=pl.DeviceIdType.MESH)

    my_rows = pl.ds(pl.multiple_of(mine * TS, TS), TS)
    loads = {}

    def load(name, src, dst, idx):
        copy = pltpu.make_async_copy(src, dst, load_sem.at[idx])
        copy.start()
        loads[name] = copy

    def dc_copy(b):
        rows = pl.ds(pl.multiple_of(b * WORDS, WORDS), WORDS)
        return pltpu.make_async_copy(dc_hbm.at[rows], dc.at[rows], dc_sem.at[b])

    def gc_copy(m):
        rows = pl.ds(pl.multiple_of(m * WORDS, WORDS), WORDS)
        return pltpu.make_async_copy(gc_hbm.at[rows], gc.at[rows], gc_sem.at[m])

    def uc_copy(m):
        rows = pl.ds(pl.multiple_of(m * WORDS, WORDS), WORDS)
        return pltpu.make_async_copy(uc_hbm.at[rows], uc.at[rows], uc_sem.at[m])

    load("ds", ds_hbm, ds, 0)
    dc_copy(0).start()
    load("og", og_hbm, og, 1)
    for b in range(1, NB):
        dc_copy(b).start()
    load("gp", gp_hbm, gp, 2)
    load("up", up_hbm, up, 3)
    load("gs", gs_hbm, gs, 4)
    load("us", us_hbm, us, 5)
    for m in range(NM):
        gc_copy(m).start()
        uc_copy(m).start()
    load("inp", inp_hbm, inp, 6)

    row = lax.broadcasted_iota(jnp.int32, (SUB, SUB), 0)
    col = lax.broadcasted_iota(jnp.int32, (SUB, SUB), 1)
    hnat[...] = (1 - 2 * parity(jnp.bitwise_and(row, col))).astype(F32).astype(BF16)
    hperm[...] = (1 - 2 * parity(jnp.bitwise_and(natural(row), col))).astype(F32).astype(BF16)
    pick[...] = (natural(row) == col).astype(F32).astype(BF16)

    def dequant(codes, scales, weights, m, base):
        for g in range(2):
            words = codes[pl.ds(pl.multiple_of(base + g * HALF, HALF), HALF), :]
            low, high = centred_pair(words)
            scale = scales[pl.ds(2 * m + g, 1), :]
            weights[m, g * HALF:(g + 1) * HALF, :] = (low * scale).astype(BF16)
            weights[m, WORDS + g * HALF:WORDS + (g + 1) * HALF, :] = (high * scale).astype(BF16)

    def p_copy(b):
        rows = pl.ds(pl.multiple_of((1 - core) * TH, TH), TH)
        return remote(pbuf.at[b, rows], prx.at[b], p_s.at[b], p_r.at[b], partner)

    def x_copy(b, k):
        rows = pl.ds(pl.multiple_of(lax.rem(x + k, NX) * TS, TS), TS)
        return remote(sbuf.at[b, rows], xrx.at[b, k - 1], x_s.at[b, k - 1], x_r.at[b, k - 1], x_dev(k))

    def y_copy(b, k):
        return remote(rg.at[0, b], rg.at[k, b], y_s.at[b, k - 1], y_r.at[b, k - 1], y_dev(k))

    def f_copy(k):
        return remote(hd.at[0], hd.at[k], f_s.at[k - 1], f_r.at[k - 1], y_dev(k))

    def first_product(b):
        dc_copy(b).wait()
        dequant(dc, ds, dw, b, b * WORDS)
        pbuf[b] = lax.dot_general(og[...], dw[b], NT, preferred_element_type=F32).astype(BF16)

    def pair_sum(b):
        p_copy(b).wait_recv()
        own = pbuf[b, pl.ds(pl.multiple_of(core * TH, TH), TH), :].astype(F32)
        sbuf[b] = (own + prx[b].astype(F32)).astype(BF16)
        for k in range(1, NX):
            x_copy(b, k).start()

    loads["ds"].wait()
    loads["og"].wait()
    first_product(0)
    pl.semaphore_wait(barrier, len(peers))
    p_copy(0).start()

    loads["gp"].wait()
    loads["up"].wait()
    gate = gp[my_rows, :].astype(F32)
    hidden = (gate * (1.0 / (1.0 + jnp.exp(-gate))) * up[my_rows, :].astype(F32)).astype(BF16)
    for b in range(NB):
        hd[0, b] = hidden[:, b * SUB:(b + 1) * SUB]
    for k in range(1, NY):
        f_copy(k).start()

    for b in range(1, NB):
        first_product(b)
        p_copy(b).start()
        pair_sum(b - 1)
    pair_sum(NB - 1)

    @pl.loop(0, T // 32)
    def _(i):
        rows = pl.ds(pl.multiple_of(i * 32, 32), 32)
        g = gp[rows, :].astype(F32)
        sg = 1.0 / (1.0 + jnp.exp(-g))
        act[rows, :] = g * sg
        slope[rows, :] = up[rows, :].astype(F32) * (sg * (1.0 + g * (1.0 - sg)))

    for b in range(NB):
        total = sbuf[b, pl.ds(pl.multiple_of(x * TS, TS), TS), :].astype(F32)
        for k in range(1, NX):
            x_copy(b, k).wait_recv()
            total = total + xrx[b, k - 1].astype(F32)
        rg[0, b] = total.astype(BF16)
        for k in range(1, NY):
            y_copy(b, k).start()

    def sign_of(k):
        source = lax.rem(y + NY - k, NY)
        both = jnp.bitwise_and(source, y)
        odd = jnp.bitwise_and(jnp.bitwise_xor(both, jnp.right_shift(both, 1)), 1)
        return (1 - 2 * odd).astype(F32)

    def rotate(parts, signs):
        turned = jnp.dot(
            parts[...].reshape(NY * NB * TS, SUB), signs[...], preferred_element_type=F32
        ).reshape(NY, NB, TS, SUB)
        total = turned[0] * sign_of(0)
        for k in range(1, NY):
            total = total + turned[k] * sign_of(k)
        pieces = [total[b] for b in range(NB)]
        step = 1
        while step < NB:
            fresh = list(pieces)
            for b in range(NB):
                if b & step:
                    fresh[b] = pieces[b - step] - pieces[b]
                else:
                    fresh[b] = pieces[b] + pieces[b + step]
            pieces = fresh
            step = step * 2
        return jnp.concatenate(pieces, axis=1) * (HB ** -0.5)

    def spread_x(buf, ssem, rsem, k):
        return remote(buf.at[mine], buf.at[mine], ssem.at[k - 1], rsem.at[k - 1], x_dev(k))

    def slot_from(k):
        return core * NX + lax.rem(x + NX - k, NX)

    def slot_of_partner(k):
        return (1 - core) * NX + lax.rem(x + NX - k, NX)

    def spread_pair(buf, ssem, rsem, k):
        slot = slot_from(k)
        return remote(buf.at[slot], buf.at[slot], ssem.at[k], rsem.at[k], partner)

    def spread(buf, xs, xr, ps, pr):
        for k in range(1, NX):
            spread_x(buf, xs, xr, k).start()
        spread_pair(buf, ps, pr, 0).start()

    for k in range(1, NY):
        f_copy(k).wait_recv()
    rta[mine] = rotate(hd, hnat).astype(BF16)
    spread(rta, ra_s, ra_r, rp_s, rp_r)

    loads["gs"].wait()
    loads["us"].wait()

    @pl.loop(0, NM)
    def _(m):
        gc_copy(m).wait()
        dequant(gc, gs, gw, m, m * WORDS)

    for b in range(NB):
        for k in range(1, NY):
            y_copy(b, k).wait_recv()
    hga[mine] = rotate(rg, hperm).astype(BF16)
    spread(hga, ga_s, ga_r, gp_s, gp_r)

    for k in range(1, NX):
        spread_x(rta, ra_s, ra_r, k).wait_recv()
        spread_pair(rta, rp_s, rp_r, k).start()

    @pl.loop(0, NM)
    def _(m):
        uc_copy(m).wait()
        dequant(uc, us, uw, m, m * WORDS)

    def grads(slot):
        rows = pl.ds(pl.multiple_of(slot * TS, TS), TS)
        hg = hga[slot].astype(F32)
        gg[rows, :] = (hg * slope[rows, :]).astype(BF16)
        ug[rows, :] = (hg * act[rows, :]).astype(BF16)

    grads(mine)
    for k in range(1, NX):
        spread_x(hga, ga_s, ga_r, k).wait_recv()
        spread_pair(hga, gp_s, gp_r, k).start()
        grads(slot_from(k))
    for k in range(NX):
        slot = slot_of_partner(k)
        remote(hga.at[slot], hga.at[slot], gp_s.at[k], gp_r.at[k], partner).wait_recv()
        grads(slot)

    def ry_copy(n, k):
        return remote(ybuf.at[n, lax.rem(y + k, NY)], yrx.at[n, k - 1], ry_s.at[n, k - 1], ry_r.at[n, k - 1], y_dev(k))

    def rz_copy(n, k):
        return remote(zbuf.at[n, lax.rem(z + k, NZ)], zrx.at[n, k - 1], rz_s.at[n, k - 1], rz_r.at[n, k - 1], z_dev(k))

    @pl.loop(0, NC)
    def _(n):
        for sub in range(2):
            m = 2 * n + sub
            both = lax.dot_general(gg[...], gw[m], NT, preferred_element_type=F32)
            both = both + lax.dot_general(ug[...], uw[m], NT, preferred_element_type=F32)
            both = both.reshape(NZ, NY, 8, SUB)
            for t in range(NY):
                ybuf[n, t, :, sub * SUB:(sub + 1) * SUB] = both[:, t].reshape(NZ * 8, SUB).astype(BF16)
        for k in range(1, NY):
            ry_copy(n, k).start()

    def y_sum(n):
        total = ybuf[n, y].astype(F32)
        for k in range(1, NY):
            ry_copy(n, k).wait_recv()
            total = total + yrx[n, k - 1].astype(F32)
        zbuf[n] = total.reshape(NZ, 8, 2 * SUB).astype(BF16)
        for k in range(1, NZ):
            rz_copy(n, k).start()

    def flip(block):
        return lax.dot_general(pick[...], block, NT, preferred_element_type=F32).astype(BF16)

    def group_sums(codes, left, right, scales, out, j, count):
        cols = pl.ds(pl.multiple_of(j * SUB, SUB), SUB)
        for m in range(count):
            full = jnp.dot(left[m], right[:, cols], preferred_element_type=F32)
            low, high = centred_pair(codes[m * WORDS:(m + 1) * WORDS, cols])
            prod = full[:WORDS] * low + full[WORDS:] * high
            for g in range(2):
                line = jnp.sum(prod[g * HALF:(g + 1) * HALF], axis=0, keepdims=True)
                out[2 * m + g:2 * m + g + 1, cols] = line * scales[2 * m + g:2 * m + g + 1, cols]

    loads["inp"].wait()
    for m in range(NM):
        xt[m] = flip(inp[:, m * SUB:(m + 1) * SUB])

    @pl.loop(0, F // SUB)
    def _(j):
        group_sums(gc, xt, gg, gs, gl_out, j, NM)

    for n in range(NC):
        y_sum(n)

    @pl.loop(0, F // SUB)
    def _(j):
        group_sums(uc, xt, ug, us, ul_out, j, NM)

    for k in range(NX):
        slot = slot_of_partner(k)
        remote(rta.at[slot], rta.at[slot], rp_s.at[k], rp_r.at[k], partner).wait_recv()
    whole = rta[...].reshape(T, F)
    for b in range(NB):
        rt[b] = flip(whole[:, b * SUB:(b + 1) * SUB])

    @pl.loop(0, D // SUB)
    def _(j):
        group_sums(dc, rt, og, ds, dl_out, j, NB)

    for n in range(NC):
        total = zbuf[n, z].astype(F32)
        for k in range(1, NZ):
            rz_copy(n, k).wait_recv()
            total = total + zrx[n, k - 1].astype(F32)
        for sub in range(2):
            unpick[2 * n + sub] = total[:, sub * SUB:(sub + 1) * SUB]
    ordered = jnp.dot(
        unpick[...].reshape(NM * 8, SUB).astype(BF16), pick[...], preferred_element_type=F32
    ).astype(BF16).astype(F32).reshape(NM, 8, SUB)
    for m in range(NM):
        gi_out[:, m * SUB:(m + 1) * SUB] = ordered[m].astype(BF16)

    for b in range(NB):
        p_copy(b).wait_send()
        for k in range(1, NX):
            x_copy(b, k).wait_send()
        for k in range(1, NY):
            y_copy(b, k).wait_send()
    for k in range(1, NY):
        f_copy(k).wait_send()
    for k in range(1, NX):
        spread_x(rta, ra_s, ra_r, k).wait_send()
        spread_x(hga, ga_s, ga_r, k).wait_send()
    for k in range(NX):
        spread_pair(rta, rp_s, rp_r, k).wait_send()
        spread_pair(hga, gp_s, gp_r, k).wait_send()
    for n in range(NC):
        for k in range(1, NY):
            ry_copy(n, k).wait_send()
        for k in range(1, NZ):
            rz_copy(n, k).wait_send()


def shards(hid, wid, inputs, gate_pre, up_pre, out_grad, gate_codes, up_codes, down_codes, gate_scale, up_scale, down_scale):
    T, D = inputs.shape
    F = gate_pre.shape[1]
    NY = HB // F
    NZ = hid // NY
    NX = wid // 2
    NB, NM = F // SUB, D // SUB
    NC = NM // 2
    TS, TH = T // wid, T // 2
    V = pltpu.VMEM
    dma = lambda *shape: pltpu.SemaphoreType.DMA(shape)
    scratch = [
        V((T, D), BF16), V((T, F), BF16), V((T, F), BF16), V((T, D), BF16),
        V((D // 2, F), jnp.int32), V((D // 2, F), jnp.int32), V((F // 2, D), jnp.int32),
        V(gate_scale.shape, F32), V(up_scale.shape, F32), V(down_scale.shape, F32),
        V((NM, SUB, F), BF16), V((NM, SUB, F), BF16), V((NB, SUB, D), BF16),
        V((T, F), F32), V((T, F), F32),
        V((NM, SUB, T), BF16), V((NB, SUB, T), BF16),
        V((T, F), BF16), V((T, F), BF16),
        V((SUB, SUB), BF16), V((SUB, SUB), BF16), V((SUB, SUB), BF16), V((NM, 8, SUB), F32),
        V((NB, T, SUB), BF16), V((NB, TH, SUB), BF16), V((NB, TH, SUB), BF16),
        V((NB, NX - 1, TS, SUB), BF16),
        V((NY, NB, TS, SUB), BF16), V((NY, NB, TS, SUB), BF16),
        V((wid, TS, F), BF16), V((wid, TS, F), BF16),
        V((NC, NY, NZ * 8, 2 * SUB), BF16), V((NC, NY - 1, NZ * 8, 2 * SUB), BF16),
        V((NC, NZ, 8, 2 * SUB), BF16), V((NC, NZ - 1, 8, 2 * SUB), BF16),
        dma(7), dma(NB), dma(NM), dma(NM),
        dma(NB), dma(NB), dma(NB, NX - 1), dma(NB, NX - 1), dma(NB, NY - 1), dma(NB, NY - 1),
        dma(NY - 1), dma(NY - 1),
        dma(NX - 1), dma(NX - 1), dma(NX), dma(NX), dma(NX - 1), dma(NX - 1), dma(NX), dma(NX),
        dma(NC, NY - 1), dma(NC, NY - 1), dma(NC, NZ - 1), dma(NC, NZ - 1),
    ]
    return pl.pallas_call(
        functools.partial(body, (NX, NY, NZ, T, D, F)),
        out_shape=(
            jax.ShapeDtypeStruct((T // hid, D), BF16),
            jax.ShapeDtypeStruct(gate_scale.shape, F32),
            jax.ShapeDtypeStruct(up_scale.shape, F32),
            jax.ShapeDtypeStruct(down_scale.shape, F32),
        ),
        in_specs=[pl.BlockSpec(memory_space=pl.ANY)] * 10,
        out_specs=[pl.BlockSpec(memory_space=pltpu.VMEM)] * 4,
        scratch_shapes=scratch,
        compiler_params=pltpu.CompilerParams(
            collective_id=0, has_side_effects=True, vmem_limit_bytes=60 * 1024 * 1024
        ),
        name="layer",
    )(inputs, gate_pre, up_pre, out_grad, gate_codes, up_codes, down_codes, gate_scale, up_scale, down_scale)


def solution(mesh):
    in_specs = (
        P(None, "wid"),
        P(None, "hid"),
        P(None, "hid"),
        P(None, "wid"),
        P("wid", "hid"),
        P("wid", "hid"),
        P("hid", "wid"),
        P("wid", "hid"),
        P("wid", "hid"),
        P("hid", "wid"),
    )
    out_specs = (P("hid", "wid"), P("wid", "hid"), P("wid", "hid"), P("hid", "wid"))
    fn = functools.partial(shards, mesh.shape["hid"], mesh.shape["wid"])
    return jax.shard_map(fn, mesh=mesh, in_specs=in_specs, out_specs=out_specs, check_vma=False)
```

time: 429 us -> 51.3 us (0.12); the launches traced: 423 us -> 51.1 us
  waiting for transfers between devices: 200 us -> 0 us
  local copies, waits for them, and re-layouts: 93.4 us -> 5.71 us
  blocking collectives: 52.2 us -> 0 us
  Pallas kernels: 0 us -> 44.7 us
  matrix products: 40.2 us -> 0 us
  other arithmetic: 19.4 us -> 0 us
  between operations: 14.3 us -> 0.64 us
    reduce_scatter x1 -> x0, waiting for transfers between devices: 157 us -> none  [shards(): lax.psum_scatter(first_term + lax.dot_general(up_grad, up_weight, contrac...]
    shift_right_arithmetic x12 -> x0, local copies, waits for them, and re-layouts: 59.2 us -> none  [unpack_centred(): jnp.right_shift(packed[:, None, :], shifts[None, :, None])]
    psum x1 -> x0, blocking collectives: 52.2 us -> none  [shards(): summed = lax.psum(partial_value, 'wid')]
    pallas_call x0 -> x1, Pallas kernels: none -> 44.7 us  [shards(): pl.pallas_call(functools.partial(body, (NX, NY, NZ, T, D, F)), out_shape=...]
    ppermute x4 -> x0, waiting for transfers between devices: 42.4 us -> none  [from_partner(): return lax.ppermute(value, axis, pairs)]
    dot_general x8 -> x0, matrix products: 40.2 us -> none  [the longest x1 8.72 us: shards(): turn_fwd = jnp.dot(hidden, signs, preferred_element_type=jnp.float32)]
    reshape x2 -> x0, local copies, waits for them, and re-layouts: 13.2 us -> none  [dequantize(): weight = (centred * jnp.repeat(scales, GROUP, axis=0)).astype(jnp.bfloat16)]
    mul x2 -> x0, local copies, waits for them, and re-layouts: 13.2 us -> none  [group_sum(): centred * values]
  transfers between devices with their start and end apart: 5 -> 0, of which waited for: 3 -> 0; matrix products, arithmetic and copies ran while one was open for 29% -> 0% of each run, Pallas kernels for 0% -> 0%
where the time goes in v1:
time: 51.3 us; the launch traced here: 51.1 us
  Pallas kernels  44.7 us (87%)
  local copies, waits for them, and re-layouts  5.71 us (11%)
  between operations  0.64 us (1%)
    pallas_call x1, Pallas kernels, shards(): pl.pallas_call(functools.partial(body, (NX, NY, NZ, T, D, F)), out_shape=...  44.7 us
    unnamed x4, local copies, waits for them, and re-layouts  5.71 us

profile of v1, /device:TPU:1, one launch (start us, length us, event | category | flops | bytes accessed | tf_op | source)
XLA Modules:
  0.0 51.1 jit_solution(10576471528136267590)
XLA Ops:
  0.6 44.7 %layer.1 = (bf16[8,1536]{1,0:T(8,128)(2,1)}, f32[12,1024]{1,0:T(8,128)}, f32[12,1024]{1,0:T(8,128)}, f32[8,1536]{1,0:T(8,128)}) custom-call(bf16[256,1536]{1,0:T(8,128)(2,1)} %inp_hbm.1, bf16[256,1024]{1,0:T(8,128)(2,1)} %gp_hbm.1, bf16[256,1024]{1,0:T(8,128)(2,1)} %up_hbm.1, bf16[256,1536]{1,0:T(8,128)(2,1)} %og_hbm.1, s32[768,1024]{1,0:T(8,128)} %gc_hbm.1, ...), custom_call_target="tpu_custom_call" | custom-call | tf_op jit(solution)/shard_map/layer/pallas_call | solution.py:417
  45.3 1.3 %copy.18 = bf16[8,1536]{1,0:T(8,128)(2,1)} copy(bf16[8,1536]{1,0:T(8,128)(2,1)} %get-tuple-element.8) | data formatting | bytes 49152
  46.7 1.5 %copy.19 = f32[12,1024]{1,0:T(8,128)} copy(f32[12,1024]{1,0:T(8,128)} %get-tuple-element.9) | data formatting | bytes 98304
  48.2 1.5 %copy.20 = f32[12,1024]{1,0:T(8,128)} copy(f32[12,1024]{1,0:T(8,128)} %get-tuple-element.10) | data formatting | bytes 98304
  49.6 1.4 %copy.21 = f32[8,1536]{1,0:T(8,128)} copy(f32[8,1536]{1,0:T(8,128)} %get-tuple-element.11) | data formatting | bytes 98304

commit v2 on v1

v2 whole, which is shorter than its diff:
```python
import functools
import jax
import jax.numpy as jnp
from jax import lax
from jax.experimental import pallas as pl
from jax.experimental.pallas import tpu as pltpu
from jax.sharding import PartitionSpec as P

HB = 4096
GROUP = 128
SUB = 256
WORDS = SUB // 2
HALF = GROUP // 2
F32 = jnp.float32
BF16 = jnp.bfloat16
NT = (((1,), (1,)), ((), ()))


def parity(v):
    v = jnp.bitwise_xor(v, jnp.right_shift(v, 4))
    v = jnp.bitwise_xor(v, jnp.right_shift(v, 2))
    v = jnp.bitwise_xor(v, jnp.right_shift(v, 1))
    return jnp.bitwise_and(v, 1)


def natural(k):
    return 2 * jnp.bitwise_and(k, WORDS - 1) + jnp.right_shift(k, 7)


def centred_pair(words):
    low = (jnp.bitwise_and(words, 15) - 8).astype(F32)
    high = (jnp.right_shift(words, 4) - 8).astype(F32)
    return low, high


def body(
    dims,
    inp_hbm, gp_hbm, up_hbm, og_hbm, gc_hbm, uc_hbm, dc_hbm, gs_hbm, us_hbm, ds_hbm,
    gi_out, gl_out, ul_out, dl_out,
    inp, gp, up, og, gc, uc, dc, gs, us, ds,
    gw, uw, dw, gwt, uwt, act, slope, xt, rt, gg, ug,
    hnat, hperm, pick, eye, unpick,
    pbuf, prx, sbuf, xrx, rg, hd, hga, rta, ybuf, yrx, zbuf, zrx,
    load_sem, dc_sem,
    p_s, p_r, x_s, x_r, y_s, y_r, f_s, f_r, ga_s, ga_r, gp_s, gp_r, ra_s, ra_r, rp_s, rp_r,
    ry_s, ry_r, rz_s, rz_r,
):
    NX, NY, NZ, T, D, F = dims
    NB = F // SUB
    NM = D // SUB
    TS = T // (2 * NX)
    TH = T // 2
    h = lax.axis_index("hid")
    w = lax.axis_index("wid")
    x = w // 2
    core = w % 2
    z = h // NY
    y = h % NY
    mine = core * NX + x

    def x_dev(k):
        return (h, lax.rem(x + k, NX) * 2 + core)

    def y_dev(k):
        return (z * NY + lax.rem(y + k, NY), w)

    def z_dev(k):
        return (lax.rem(z + k, NZ) * NY + y, w)

    partner = (h, x * 2 + 1 - core)
    near = [1, NX - 1] if NX > 2 else []
    far = NX // 2

    def remote(src, dst, ssem, rsem, dev):
        return pltpu.make_async_remote_copy(
            src_ref=src, dst_ref=dst, send_sem=ssem, recv_sem=rsem,
            device_id=dev, device_id_type=pl.DeviceIdType.MESH,
        )

    def all_of(ref, sem):
        pltpu.make_async_copy(ref, ref, sem).wait()

    barrier = pltpu.get_barrier_semaphore()
    peers = [partner] + [x_dev(k) for k in range(1, NX)] + [y_dev(k) for k in range(1, NY)]
    peers += [z_dev(k) for k in range(1, NZ)]
    for dev in peers:
        pl.semaphore_signal(barrier, inc=1, device_id=dev, device_id_type=pl.DeviceIdType.MESH)

    my_rows = pl.ds(pl.multiple_of(mine * TS, TS), TS)
    loads = {}

    def load(name, src, dst, idx):
        copy = pltpu.make_async_copy(src, dst, load_sem.at[idx])
        copy.start()
        loads[name] = copy

    def dc_copy(b):
        rows = pl.ds(pl.multiple_of(b * WORDS, WORDS), WORDS)
        return pltpu.make_async_copy(dc_hbm.at[rows], dc.at[rows], dc_sem.at[b])

    load("ds", ds_hbm, ds, 0)
    dc_copy(0).start()
    load("og", og_hbm, og, 1)
    for b in range(1, NB):
        dc_copy(b).start()
    load("gp", gp_hbm, gp, 2)
    load("up", up_hbm, up, 3)

    row = lax.broadcasted_iota(jnp.int32, (SUB, SUB), 0)
    col = lax.broadcasted_iota(jnp.int32, (SUB, SUB), 1)
    hnat[...] = (1 - 2 * parity(jnp.bitwise_and(row, col))).astype(F32).astype(BF16)
    hperm[...] = (1 - 2 * parity(jnp.bitwise_and(natural(row), col))).astype(F32).astype(BF16)
    eye[...] = (row == col).astype(F32).astype(BF16)
    pick[...] = (natural(row) == col).astype(F32).astype(BF16)

    def dequant(codes, scales, weights, m, base):
        for g in range(2):
            words = codes[base + g * HALF:base + (g + 1) * HALF, :]
            low, high = centred_pair(words)
            scale = scales[2 * m + g:2 * m + g + 1, :]
            weights[m, g * HALF:(g + 1) * HALF, :] = (low * scale).astype(BF16)
            weights[m, WORDS + g * HALF:WORDS + (g + 1) * HALF, :] = (high * scale).astype(BF16)

    def p_copy(b):
        rows = pl.ds(pl.multiple_of((1 - core) * TH, TH), TH)
        return remote(pbuf.at[b, rows], prx.at[b], p_s, p_r.at[b], partner)

    def x_copy(b, k):
        rows = pl.ds(pl.multiple_of(lax.rem(x + k, NX) * TS, TS), TS)
        return remote(sbuf.at[b, rows], xrx.at[b, k - 1], x_s, x_r.at[b], x_dev(k))

    def y_copy(b, k):
        return remote(rg.at[0, b], rg.at[k, b], y_s, y_r, y_dev(k))

    def f_copy(k):
        return remote(hd.at[0], hd.at[k], f_s, f_r, y_dev(k))

    def first_product(b):
        if b:
            dc_copy(b).wait()
        dequant(dc, ds, dw, b, b * WORDS)
        pbuf[b] = lax.dot_general(og[...], dw[b], NT, preferred_element_type=F32).astype(BF16)

    def pair_sum(b):
        p_copy(b).wait_recv()
        own = pbuf[b, pl.ds(pl.multiple_of(core * TH, TH), TH), :].astype(F32)
        sbuf[b] = (own + prx[b].astype(F32)).astype(BF16)
        for k in range(1, NX):
            x_copy(b, k).start()

    loads["ds"].wait()
    loads["og"].wait()
    dc_copy(0).wait()
    first_product(0)
    load("gs", gs_hbm, gs, 4)
    load("us", us_hbm, us, 5)
    load("gc", gc_hbm, gc, 7)
    load("uc", uc_hbm, uc, 8)
    load("inp", inp_hbm, inp, 6)
    pl.semaphore_wait(barrier, len(peers))
    p_copy(0).start()

    loads["gp"].wait()
    loads["up"].wait()
    gate = gp[my_rows, :].astype(F32)
    hidden = (gate * (1.0 / (1.0 + jnp.exp(-gate))) * up[my_rows, :].astype(F32)).astype(BF16)
    for b in range(NB):
        hd[0, b] = hidden[:, b * SUB:(b + 1) * SUB]
    for k in range(1, NY):
        f_copy(k).start()

    for b in range(1, NB):
        first_product(b)
        p_copy(b).start()
        if b >= 2:
            pair_sum(b - 2)
    pair_sum(NB - 2)
    pair_sum(NB - 1)

    @pl.loop(0, T // 32)
    def _(i):
        rows = pl.ds(pl.multiple_of(i * 32, 32), 32)
        g = gp[rows, :].astype(F32)
        sg = 1.0 / (1.0 + jnp.exp(-g))
        act[rows, :] = g * sg
        slope[rows, :] = up[rows, :].astype(F32) * (sg * (1.0 + g * (1.0 - sg)))

    def sign_of(k):
        source = lax.rem(y + NY - k, NY)
        both = jnp.bitwise_and(source, y)
        odd = jnp.bitwise_and(jnp.bitwise_xor(both, jnp.right_shift(both, 1)), 1)
        return (1 - 2 * odd).astype(F32)

    def rotate(parts, signs):
        turned = jnp.dot(
            parts[...].reshape(NY * NB * TS, SUB), signs[...], preferred_element_type=F32
        ).reshape(NY, NB, TS, SUB)
        total = turned[0] * sign_of(0)
        for k in range(1, NY):
            total = total + turned[k] * sign_of(k)
        pieces = [total[b] for b in range(NB)]
        step = 1
        while step < NB:
            fresh = list(pieces)
            for b in range(NB):
                if b & step:
                    fresh[b] = pieces[b - step] - pieces[b]
                else:
                    fresh[b] = pieces[b] + pieces[b + step]
            pieces = fresh
            step = step * 2
        return jnp.concatenate(pieces, axis=1) * (HB ** -0.5)

    def spread_x(buf, ssem, rsem, k):
        return remote(buf.at[mine], buf.at[mine], ssem, rsem, x_dev(k))

    def slot_from(k):
        return core * NX + lax.rem(x + NX - k, NX)

    def slot_of_partner(k):
        return (1 - core) * NX + lax.rem(x + NX - k, NX)

    def spread_pair(buf, ssem, rsem, k):
        slot = slot_from(k)
        return remote(buf.at[slot], buf.at[slot], ssem, rsem, partner)

    def spread(buf, xs, xr, ps, pr):
        for k in near + [far]:
            spread_x(buf, xs, xr(k), k).start()
        spread_pair(buf, ps, pr(0), 0).start()

    loads["gs"].wait()
    loads["us"].wait()
    loads["gc"].wait()

    def turn(weights, turned, m):
        for f in range(F // SUB):
            block = weights[m, :, f * SUB:(f + 1) * SUB]
            across = lax.dot_general(eye[...], block, NT, preferred_element_type=F32)
            turned[f * SUB:(f + 1) * SUB, m * SUB:(m + 1) * SUB] = across.astype(BF16)

    def prepare(codes, scales, weights, turned):
        for m in range(NM):
            dequant(codes, scales, weights, m, m * WORDS)
            if m:
                turn(weights, turned, m - 1)
        turn(weights, turned, NM - 1)

    prepare(gc, gs, gw, gwt)

    all_of(hd.at[pl.ds(1, NY - 1)], f_r)
    rta[mine] = rotate(hd, hnat).astype(BF16)
    spread(rta, ra_s, lambda k: ra_r, rp_s, lambda k: rp_r)

    for b in range(NB):
        total = sbuf[b, pl.ds(pl.multiple_of(x * TS, TS), TS), :].astype(F32)
        all_of(xrx.at[b], x_r.at[b])
        for k in range(1, NX):
            total = total + xrx[b, k - 1].astype(F32)
        rg[0, b] = total.astype(BF16)
        for k in range(1, NY):
            y_copy(b, k).start()

    def flip(block):
        return lax.dot_general(pick[...], block, NT, preferred_element_type=F32).astype(BF16)

    def group_sums(codes, left, right, scales, out, j, count):
        cols = pl.ds(pl.multiple_of(j * SUB, SUB), SUB)
        for m in range(count):
            full = jnp.dot(left[m], right[:, cols], preferred_element_type=F32)
            low, high = centred_pair(codes[m * WORDS:(m + 1) * WORDS, cols])
            prod = full[:WORDS] * low + full[WORDS:] * high
            for g in range(2):
                line = jnp.sum(prod[g * HALF:(g + 1) * HALF], axis=0, keepdims=True)
                out[2 * m + g:2 * m + g + 1, cols] = line * scales[2 * m + g:2 * m + g + 1, cols]

    loads["uc"].wait()
    prepare(uc, us, uw, uwt)

    all_of(rg.at[pl.ds(1, NY - 1)], y_r)
    hga[mine] = rotate(rg, hperm).astype(BF16)
    spread(hga, ga_s, lambda k: ga_r.at[k - 1], gp_s, lambda k: gp_r.at[k])

    def ry_copy(slot, half, k):
        cols = pl.ds(half * D // 2, D // 2)
        return remote(
            ybuf.at[slot, lax.rem(y + k, NY), :, cols], yrx.at[slot, k - 1, :, cols],
            ry_s, ry_r.at[slot], y_dev(k),
        )

    def rz_copy(k):
        return remote(zbuf.at[lax.rem(z + k, NZ)], zrx.at[k - 1], rz_s, rz_r, z_dev(k))

    def slot_rows(slot):
        return pl.ds(pl.multiple_of(slot * TS, TS), TS)

    def factors(slots):
        for slot in slots:
            rows = slot_rows(slot)
            hg = hga[slot].astype(F32)
            gg[rows, :] = (hg * slope[rows, :]).astype(BF16)
            ug[rows, :] = (hg * act[rows, :]).astype(BF16)

    def products(slots, half):
        for m in range(half * NM // 2, (half + 1) * NM // 2):
            left = jnp.concatenate([gg[slot_rows(slot), :] for slot in slots], axis=0)
            both = jnp.dot(left, gwt[:, m * SUB:(m + 1) * SUB], preferred_element_type=F32)
            left = jnp.concatenate([ug[slot_rows(slot), :] for slot in slots], axis=0)
            both = both + jnp.dot(left, uwt[:, m * SUB:(m + 1) * SUB], preferred_element_type=F32)
            for i, slot in enumerate(slots):
                piece = both[i * TS:(i + 1) * TS].reshape(NY, 8, SUB).astype(BF16)
                ybuf[slot, :, :, m * SUB:(m + 1) * SUB] = piece
        for slot in slots:
            for k in range(1, NY):
                ry_copy(slot, half, k).start()

    def y_sum(slot):
        total = ybuf[slot, y].astype(F32)
        all_of(yrx.at[slot], ry_r.at[slot])
        for k in range(1, NY):
            total = total + yrx[slot, k - 1].astype(F32)
        zbuf[slot] = total.astype(BF16)

        @pl.when(slot != z)
        def _():
            rz_copy(lax.rem(slot - z + NZ, NZ)).start()

    def from_x(k):
        spread_x(hga, ga_s, ga_r.at[k - 1], k).wait_recv()
        spread_pair(hga, gp_s, gp_r.at[k], k).start()

    def from_pair(k):
        slot = slot_of_partner(k)
        remote(hga.at[slot], hga.at[slot], gp_s, gp_r.at[k], partner).wait_recv()


    all_of(rta.at[pl.ds(0, NX - 1)], ra_r)
    for k in range(1, NX):
        spread_pair(rta, rp_s, rp_r, k).start()
    loads["inp"].wait()
    for m in range(NM):
        xt[m] = flip(inp[:, m * SUB:(m + 1) * SUB])
    first = [mine, slot_of_partner(0)]
    second = [slot_from(k) for k in near]
    third = [slot_of_partner(k) for k in near] + [slot_from(far), slot_of_partner(far)]
    groups = [first, second, third] if near else [first, third]
    from_pair(0)
    factors(first)
    products(first, 0)
    products(first, 1)
    for k in near:
        from_x(k)
    if near:
        factors(second)
        products(second, 0)
    from_x(far)
    if near:
        products(second, 1)
    for k in near:
        from_pair(k)
    from_pair(far)
    factors(third)
    products(third, 0)
    products(third, 1)

    def y_sums(i):
        if i < len(groups):
            for slot in groups[i]:
                y_sum(slot)

    y_sums(0)
    all_of(rta.at[pl.ds(0, NX)], rp_r)
    whole = rta[...].reshape(T, F)
    for b in range(NB):
        rt[b] = flip(whole[:, b * SUB:(b + 1) * SUB])

    @pl.loop(0, D // SUB)
    def _(j):
        group_sums(dc, rt, og, ds, dl_out, j, NB)

    y_sums(1)
    @pl.loop(0, F // SUB)
    def _(j):
        group_sums(gc, xt, gg, gs, gl_out, j, NM)

    y_sums(2)
    @pl.loop(0, F // SUB)
    def _(j):
        group_sums(uc, xt, ug, us, ul_out, j, NM)

    total = zbuf[z].astype(F32)
    all_of(zrx, rz_r)
    for k in range(1, NZ):
        total = total + zrx[k - 1].astype(F32)
    for m in range(NM):
        unpick[m] = total[:, m * SUB:(m + 1) * SUB]
    ordered = jnp.dot(
        unpick[...].reshape(NM * 8, SUB).astype(BF16), pick[...], preferred_element_type=F32
    ).astype(BF16).astype(F32).reshape(NM, 8, SUB)
    for m in range(NM):
        gi_out[:, m * SUB:(m + 1) * SUB] = ordered[m].astype(BF16)

    all_of(prx, p_s)
    all_of(xrx, x_s)
    all_of(rg.at[pl.ds(1, NY - 1)], y_s)
    all_of(hd.at[pl.ds(1, NY - 1)], f_s)
    all_of(rta.at[pl.ds(0, NX - 1)], ra_s)
    all_of(hga.at[pl.ds(0, NX - 1)], ga_s)
    all_of(rta.at[pl.ds(0, NX)], rp_s)
    all_of(hga.at[pl.ds(0, NX)], gp_s)
    all_of(yrx, ry_s)
    all_of(zrx, rz_s)


def hand_out(*refs):
    sem = refs[8]
    copies = [pltpu.make_async_copy(refs[i], refs[4 + i], sem.at[i]) for i in range(4)]
    for copy in copies:
        copy.start()
    for copy in copies:
        copy.wait()


def shards(hid, wid, inputs, gate_pre, up_pre, out_grad, gate_codes, up_codes, down_codes, gate_scale, up_scale, down_scale):
    T, D = inputs.shape
    F = gate_pre.shape[1]
    NY = HB // F
    NZ = hid // NY
    NX = wid // 2
    NB, NM = F // SUB, D // SUB
    TS, TH = T // wid, T // 2
    V = pltpu.VMEM
    dma = lambda *shape: pltpu.SemaphoreType.DMA(shape)
    one = pltpu.SemaphoreType.DMA
    scratch = [
        V((T, D), BF16), V((T, F), BF16), V((T, F), BF16), V((T, D), BF16),
        V((D // 2, F), jnp.int32), V((D // 2, F), jnp.int32), V((F // 2, D), jnp.int32),
        V(gate_scale.shape, F32), V(up_scale.shape, F32), V(down_scale.shape, F32),
        V((NM, SUB, F), BF16), V((NM, SUB, F), BF16), V((NB, SUB, D), BF16), V((F, D), BF16), V((F, D), BF16),
        V((T, F), F32), V((T, F), F32),
        V((NM, SUB, T), BF16), V((NB, SUB, T), BF16),
        V((T, F), BF16), V((T, F), BF16),
        V((SUB, SUB), BF16), V((SUB, SUB), BF16), V((SUB, SUB), BF16), V((SUB, SUB), BF16), V((NM, 8, SUB), F32),
        V((NB, T, SUB), BF16), V((NB, TH, SUB), BF16), V((NB, TH, SUB), BF16),
        V((NB, NX - 1, TS, SUB), BF16),
        V((NY, NB, TS, SUB), BF16), V((NY, NB, TS, SUB), BF16),
        V((wid, TS, F), BF16), V((wid, TS, F), BF16),
        V((wid, NY, 8, D), BF16), V((wid, NY - 1, 8, D), BF16),
        V((NZ, 8, D), BF16), V((NZ - 1, 8, D), BF16),
        dma(9), dma(NB),
        one, dma(NB), one, dma(NB), one, one, one, one,
        one, dma(NX - 1), one, dma(NX), one, one, one, one,
        one, dma(wid), one, one,
    ]
    results = pl.pallas_call(
        functools.partial(body, (NX, NY, NZ, T, D, F)),
        out_shape=(
            V((T // hid, D), BF16), V(gate_scale.shape, F32), V(up_scale.shape, F32), V(down_scale.shape, F32),
        ),
        in_specs=[pl.BlockSpec(memory_space=pl.ANY)] * 10,
        out_specs=[pl.BlockSpec(memory_space=pltpu.VMEM)] * 4,
        scratch_shapes=scratch,
        compiler_params=pltpu.CompilerParams(
            collective_id=0, has_side_effects=True, vmem_limit_bytes=60 * 1024 * 1024
        ),
        name="layer",
    )(inputs, gate_pre, up_pre, out_grad, gate_codes, up_codes, down_codes, gate_scale, up_scale, down_scale)
    return pl.pallas_call(
        hand_out,
        out_shape=[jax.ShapeDtypeStruct(r.shape, r.dtype) for r in results],
        in_specs=[pl.BlockSpec(memory_space=pltpu.VMEM)] * 4,
        out_specs=[pl.BlockSpec(memory_space=pl.ANY)] * 4,
        scratch_shapes=[dma(4)],
        name="hand_out",
    )(*[pltpu.with_memory_space_constraint(r, pltpu.VMEM) for r in results])


def solution(mesh):
    in_specs = (
        P(None, "wid"),
        P(None, "hid"),
        P(None, "hid"),
        P(None, "wid"),
        P("wid", "hid"),
        P("wid", "hid"),
        P("hid", "wid"),
        P("wid", "hid"),
        P("wid", "hid"),
        P("hid", "wid"),
    )
    out_specs = (P("hid", "wid"), P("wid", "hid"), P("wid", "hid"), P("hid", "wid"))
    fn = functools.partial(shards, mesh.shape["hid"], mesh.shape["wid"])
    return jax.shard_map(fn, mesh=mesh, in_specs=in_specs, out_specs=out_specs, check_vma=False)
```

time: 51.3 us -> 39.6 us (0.77)
  Pallas kernels: 44.7 us -> 38.4 us
  local copies, waits for them, and re-layouts: 5.71 us -> 0 us
    pallas_call x1, Pallas kernels: 44.7 us -> 37.7 us  [shards(): pl.pallas_call(functools.partial(body, (NX, NY, NZ, T, D, F)), out_shape=...]
    unnamed x4 -> x0, local copies, waits for them, and re-layouts: 5.71 us -> none
    pallas_call x0 -> x1, Pallas kernels: none -> 0.71 us  [shards(): pl.pallas_call(hand_out, out_shape=[jax.ShapeDtypeStruct(r.shape, r.dtype...]
where the time goes in v2:
time: 39.6 us; the launch traced here: 39 us
  Pallas kernels  38.4 us (97%)
  between operations  0.64 us (2%)
    pallas_call x1, Pallas kernels, shards(): pl.pallas_call(functools.partial(body, (NX, NY, NZ, T, D, F)), out_shape=...  37.7 us

profile of v2, /device:TPU:1, one launch (start us, length us, event | category | flops | bytes accessed | tf_op | source)
XLA Modules:
  0.0 39.0 jit_solution(6946038400369410752)
XLA Ops:
  0.6 37.7 %layer.1 = (bf16[8,1536]{1,0:T(8,128)(2,1)S(1)}, f32[12,1024]{1,0:T(8,128)S(1)}, f32[12,1024]{1,0:T(8,128)S(1)}, f32[8,1536]{1,0:T(8,128)S(1)}) custom-call(bf16[256,1536]{1,0:T(8,128)(2,1)} %inp_hbm.1, bf16[256,1024]{1,0:T(8,128)(2,1)} %gp_hbm.1, bf16[256,1024]{1,0:T(8,128)(2,1)} %up_hbm.1, bf16[256,1536]{1,0:T(8,128)(2,1)} %og_hbm.1, s32[768,1024]{1,0:T(8,128)} %gc_hbm.1, ...), custom_call_target="tpu_custom_call" | custom-call | tf_op jit(solution)/shard_map/layer/pallas_call | solution.py:455
  38.3 0.7 %hand_out.1 = (bf16[8,1536]{1,0:T(8,128)(2,1)}, f32[12,1024]{1,0:T(8,128)}, f32[12,1024]{1,0:T(8,128)}, f32[8,1536]{1,0:T(8,128)}) custom-call(bf16[8,1536]{1,0:T(8,128)(2,1)S(1)} %get-tuple-element.8.refs_0_, f32[12,1024]{1,0:T(8,128)S(1)} %get-tuple-element.9.refs_1_, f32[12,1024]{1,0:T(8,128)S(1)} %get-tuple-element.10.refs_2_, ...), custom_call_target="tpu_custom_call" | custom-call | tf_op jit(solution)/shard_map/hand_out/pallas_call | solution.py:468

commit v3 on v2

--- a/solution.py
+++ b/solution.py
@@ -145,7 +145,7 @@
         p_copy(b).wait_recv()
         own = pbuf[b, pl.ds(pl.multiple_of(core * TH, TH), TH), :].astype(F32)
         sbuf[b] = (own + prx[b].astype(F32)).astype(BF16)
-        for k in range(1, NX):
+        for k in [far] + near:
             x_copy(b, k).start()
 
     loads["ds"].wait()
@@ -225,7 +225,7 @@
         return remote(buf.at[slot], buf.at[slot], ssem, rsem, partner)
 
     def spread(buf, xs, xr, ps, pr):
-        for k in near + [far]:
+        for k in near:
             spread_x(buf, xs, xr(k), k).start()
         spread_pair(buf, ps, pr(0), 0).start()
 
@@ -248,17 +248,13 @@
 
     prepare(gc, gs, gw, gwt)
 
-    all_of(hd.at[pl.ds(1, NY - 1)], f_r)
-    rta[mine] = rotate(hd, hnat).astype(BF16)
-    spread(rta, ra_s, lambda k: ra_r, rp_s, lambda k: rp_r)
-
     for b in range(NB):
         total = sbuf[b, pl.ds(pl.multiple_of(x * TS, TS), TS), :].astype(F32)
         all_of(xrx.at[b], x_r.at[b])
         for k in range(1, NX):
             total = total + xrx[b, k - 1].astype(F32)
         rg[0, b] = total.astype(BF16)
-        for k in range(1, NY):
+        for k in [2, 1, 3]:
             y_copy(b, k).start()
 
     def flip(block):
@@ -274,6 +270,11 @@
                 line = jnp.sum(prod[g * HALF:(g + 1) * HALF], axis=0, keepdims=True)
                 out[2 * m + g:2 * m + g + 1, cols] = line * scales[2 * m + g:2 * m + g + 1, cols]
 
+    all_of(hd.at[pl.ds(1, NY - 1)], f_r)
+    rta[mine] = rotate(hd, hnat).astype(BF16)
+    spread(rta, ra_s, lambda k: ra_r, rp_s, lambda k: rp_r)
+    spread_x(rta, ra_s, ra_r, far).start()
+
     loads["uc"].wait()
     prepare(uc, us, uw, uwt)
 
@@ -281,15 +282,19 @@
     hga[mine] = rotate(rg, hperm).astype(BF16)
     spread(hga, ga_s, lambda k: ga_r.at[k - 1], gp_s, lambda k: gp_r.at[k])
 
-    def ry_copy(slot, half, k):
-        cols = pl.ds(half * D // 2, D // 2)
+    def part_cols(part, parts):
+        return pl.ds(part * D // parts, D // parts)
+
+    def ry_copy(slot, cols, sem, k):
         return remote(
             ybuf.at[slot, lax.rem(y + k, NY), :, cols], yrx.at[slot, k - 1, :, cols],
-            ry_s, ry_r.at[slot], y_dev(k),
+            ry_s, ry_r.at[sem], y_dev(k),
         )
 
-    def rz_copy(k):
-        return remote(zbuf.at[lax.rem(z + k, NZ)], zrx.at[k - 1], rz_s, rz_r, z_dev(k))
+    def rz_copy(k, cols):
+        return remote(
+            zbuf.at[lax.rem(z + k, NZ), :, cols], zrx.at[k - 1, :, cols], rz_s, rz_r, z_dev(k)
+        )
 
     def slot_rows(slot):
         return pl.ds(pl.multiple_of(slot * TS, TS), TS)
@@ -301,8 +306,8 @@
             gg[rows, :] = (hg * slope[rows, :]).astype(BF16)
             ug[rows, :] = (hg * act[rows, :]).astype(BF16)
 
-    def products(slots, half):
-        for m in range(half * NM // 2, (half + 1) * NM // 2):
+    def products(slots, part, parts, sem):
+        for m in range(part * NM // parts, (part + 1) * NM // parts):
             left = jnp.concatenate([gg[slot_rows(slot), :] for slot in slots], axis=0)
             both = jnp.dot(left, gwt[:, m * SUB:(m + 1) * SUB], preferred_element_type=F32)
             left = jnp.concatenate([ug[slot_rows(slot), :] for slot in slots], axis=0)
@@ -311,19 +316,21 @@
                 piece = both[i * TS:(i + 1) * TS].reshape(NY, 8, SUB).astype(BF16)
                 ybuf[slot, :, :, m * SUB:(m + 1) * SUB] = piece
         for slot in slots:
+            for k in [2, 1, 3]:
+                ry_copy(slot, part_cols(part, parts), sem, k).start()
+
+    def y_sums(slots, part, parts, sem):
+        cols = part_cols(part, parts)
+        all_of(yrx.at[pl.ds(0, len(slots)), :, :, cols], ry_r.at[sem])
+        for slot in slots:
+            total = ybuf[slot, y, :, cols].astype(F32)
             for k in range(1, NY):
-                ry_copy(slot, half, k).start()
-
-    def y_sum(slot):
-        total = ybuf[slot, y].astype(F32)
-        all_of(yrx.at[slot], ry_r.at[slot])
-        for k in range(1, NY):
-            total = total + yrx[slot, k - 1].astype(F32)
-        zbuf[slot] = total.astype(BF16)
-
-        @pl.when(slot != z)
-        def _():
-            rz_copy(lax.rem(slot - z + NZ, NZ)).start()
+                total = total + yrx[slot, k - 1, :, cols].astype(F32)
+            zbuf[slot, :, cols] = total.astype(BF16)
+
+            @pl.when(slot != z)
+            def _():
+                rz_copy(lax.rem(slot - z + NZ, NZ), cols).start()
 
     def from_x(k):
         spread_x(hga, ga_s, ga_r.at[k - 1], k).wait_recv()
@@ -334,59 +341,69 @@
         remote(hga.at[slot], hga.at[slot], gp_s, gp_r.at[k], partner).wait_recv()
 
 
-    all_of(rta.at[pl.ds(0, NX - 1)], ra_r)
-    for k in range(1, NX):
-        spread_pair(rta, rp_s, rp_r, k).start()
     loads["inp"].wait()
     for m in range(NM):
         xt[m] = flip(inp[:, m * SUB:(m + 1) * SUB])
     first = [mine, slot_of_partner(0)]
     second = [slot_from(k) for k in near]
-    third = [slot_of_partner(k) for k in near] + [slot_from(far), slot_of_partner(far)]
-    groups = [first, second, third] if near else [first, third]
+    third = [slot_of_partner(k) for k in near]
+    fourth = [slot_from(far), slot_of_partner(far)]
     from_pair(0)
+    spread_x(hga, ga_s, ga_r.at[far - 1], far).start()
     factors(first)
-    products(first, 0)
-    products(first, 1)
+    products(first, 0, 2, 0)
+    products(first, 1, 2, 0)
+    all_of(rta.at[pl.ds(0, NX - 1)], ra_r)
+    for k in range(1, NX):
+        spread_pair(rta, rp_s, rp_r, k).start()
     for k in near:
         from_x(k)
     if near:
         factors(second)
-        products(second, 0)
+        for part in range(2):
+            products(second, part, 2, 1)
+    for k in near:
+        from_pair(k)
+    if near:
+        factors(third)
+        products(third, 0, 2, 2)
     from_x(far)
     if near:
-        products(second, 1)
-    for k in near:
-        from_pair(k)
+        products(third, 1, 2, 2)
+    y_sums(first, 0, 1, 0)
     from_pair(far)
-    factors(third)
-    products(third, 0)
-    products(third, 1)
-
-    def y_sums(i):
-        if i < len(groups):
-            for slot in groups[i]:
-                y_sum(slot)
-
-    y_sums(0)
+    factors(fourth)
+    for part in range(2):
+        products(fourth, part, 2, 3 + part)
+
     all_of(rta.at[pl.ds(0, NX)], rp_r)
     whole = rta[...].reshape(T, F)
     for b in range(NB):
         rt[b] = flip(whole[:, b * SUB:(b + 1) * SUB])
 
-    @pl.loop(0, D // SUB)
-    def _(j):
-        group_sums(dc, rt, og, ds, dl_out, j, NB)
-
-    y_sums(1)
-    @pl.loop(0, F // SUB)
-    def _(j):
-        group_sums(gc, xt, gg, gs, gl_out, j, NM)
-
-    y_sums(2)
-    @pl.loop(0, F // SUB)
-    def _(j):
-        group_sums(uc, xt, ug, us, ul_out, j, NM)
+    def sums_over(*args):
+        def run(start, stop):
+            @pl.loop(start, stop)
+            def _(j):
+                group_sums(*args[:5], j, args[5])
+
+        return run
+
+    down_sums = sums_over(dc, rt, og, ds, dl_out, NB)
+    gate_sums = sums_over(gc, xt, gg, gs, gl_out, NM)
+    up_sums = sums_over(uc, xt, ug, us, ul_out, NM)
+    blocks = F // SUB
+
+    if near:
+        y_sums(second, 0, 1, 1)
+    down_sums(0, NM)
+    if near:
+        y_sums(third, 0, 1, 2)
+    gate_sums(0, blocks // 2)
+    y_sums(fourth, 0, 2, 3)
+    gate_sums(blocks // 2, blocks)
+    y_sums(fourth, 1, 2, 4)
+    up_sums(0, blocks)
 
     total = zbuf[z].astype(F32)
     all_of(zrx, rz_r)
@@ -450,7 +467,7 @@
         dma(9), dma(NB),
         one, dma(NB), one, dma(NB), one, one, one, one,
         one, dma(NX - 1), one, dma(NX), one, one, one, one,
-        one, dma(wid), one, one,
+        one, dma(5), one, one,
     ]
     results = pl.pallas_call(
         functools.partial(body, (NX, NY, NZ, T, D, F)),

time: 39.6 us -> 38.3 us (0.967); the launches traced: 39 us -> 38.2 us
  Pallas kernels: 38.4 us -> 37.6 us
    pallas_call x1, Pallas kernels: 37.7 us -> 36.9 us  [shards(): pl.pallas_call(functools.partial(body, (NX, NY, NZ, T, D, F)), out_shape=...]
where the time goes in v3:
time: 38.3 us; the launch traced here: 38.2 us
  Pallas kernels  37.6 us (98%)
  between operations  0.64 us (2%)
    pallas_call x1, Pallas kernels, shards(): pl.pallas_call(functools.partial(body, (NX, NY, NZ, T, D, F)), out_shape=...  36.9 us

profile of v3, /device:TPU:1, one launch (start us, length us, event | category | flops | bytes accessed | tf_op | source)
XLA Modules:
  0.0 38.2 jit_solution(16106069464084611506)
XLA Ops:
  0.6 36.9 %layer.1 = (bf16[8,1536]{1,0:T(8,128)(2,1)S(1)}, f32[12,1024]{1,0:T(8,128)S(1)}, f32[12,1024]{1,0:T(8,128)S(1)}, f32[8,1536]{1,0:T(8,128)S(1)}) custom-call(bf16[256,1536]{1,0:T(8,128)(2,1)} %inp_hbm.1, bf16[256,1024]{1,0:T(8,128)(2,1)} %gp_hbm.1, bf16[256,1024]{1,0:T(8,128)(2,1)} %up_hbm.1, bf16[256,1536]{1,0:T(8,128)(2,1)} %og_hbm.1, s32[768,1024]{1,0:T(8,128)} %gc_hbm.1, ...), custom_call_target="tpu_custom_call" | custom-call | tf_op jit(solution)/shard_map/layer/pallas_call | solution.py:472
  37.5 0.7 %hand_out.1 = (bf16[8,1536]{1,0:T(8,128)(2,1)}, f32[12,1024]{1,0:T(8,128)}, f32[12,1024]{1,0:T(8,128)}, f32[8,1536]{1,0:T(8,128)}) custom-call(bf16[8,1536]{1,0:T(8,128)(2,1)S(1)} %get-tuple-element.8.refs_0_, f32[12,1024]{1,0:T(8,128)S(1)} %get-tuple-element.9.refs_1_, f32[12,1024]{1,0:T(8,128)S(1)} %get-tuple-element.10.refs_2_, ...), custom_call_target="tpu_custom_call" | custom-call | tf_op jit(solution)/shard_map/hand_out/pallas_call | solution.py:485

commit v4 on v3

--- a/solution.py
+++ b/solution.py
@@ -41,7 +41,7 @@
     gw, uw, dw, gwt, uwt, act, slope, xt, rt, gg, ug,
     hnat, hperm, pick, eye, unpick,
     pbuf, prx, sbuf, xrx, rg, hd, hga, rta, ybuf, yrx, zbuf, zrx,
-    load_sem, dc_sem,
+    plane_in, line_in, load_sem, dc_sem,
     p_s, p_r, x_s, x_r, y_s, y_r, f_s, f_r, ga_s, ga_r, gp_s, gp_r, ra_s, ra_r, rp_s, rp_r,
     ry_s, ry_r, rz_s, rz_r,
 ):
@@ -81,10 +81,16 @@
         pltpu.make_async_copy(ref, ref, sem).wait()
 
     barrier = pltpu.get_barrier_semaphore()
-    peers = [partner] + [x_dev(k) for k in range(1, NX)] + [y_dev(k) for k in range(1, NY)]
-    peers += [z_dev(k) for k in range(1, NZ)]
-    for dev in peers:
-        pl.semaphore_signal(barrier, inc=1, device_id=dev, device_id_type=pl.DeviceIdType.MESH)
+    def tell(sem, dev):
+        pl.semaphore_signal(sem, inc=1, device_id=dev, device_id_type=pl.DeviceIdType.MESH)
+
+    tell(barrier, partner)
+    for k in range(1, NX):
+        tell(barrier, (h, lax.rem(x + k, NX) * 2))
+    for k in range(1, NY):
+        tell(barrier, (z * NY + lax.rem(y + k, NY), 2 * x))
+    for k in range(1, NZ):
+        tell(barrier, (lax.rem(z + k, NZ) * NY + y, 2 * x + 1))
 
     my_rows = pl.ds(pl.multiple_of(mine * TS, TS), TS)
     loads = {}
@@ -157,7 +163,15 @@
     load("gc", gc_hbm, gc, 7)
     load("uc", uc_hbm, uc, 8)
     load("inp", inp_hbm, inp, 6)
-    pl.semaphore_wait(barrier, len(peers))
+    @pl.when(core == 0)
+    def _():
+        pl.semaphore_wait(barrier, 2 * (NX + NY - 2) + 1)
+        tell(plane_in, partner)
+
+    @pl.when(core == 1)
+    def _():
+        pl.semaphore_wait(plane_in, 1)
+
     p_copy(0).start()
 
     loads["gp"].wait()
@@ -306,7 +320,7 @@
             gg[rows, :] = (hg * slope[rows, :]).astype(BF16)
             ug[rows, :] = (hg * act[rows, :]).astype(BF16)
 
-    def products(slots, part, parts, sem):
+    def products(slots, part, parts):
         for m in range(part * NM // parts, (part + 1) * NM // parts):
             left = jnp.concatenate([gg[slot_rows(slot), :] for slot in slots], axis=0)
             both = jnp.dot(left, gwt[:, m * SUB:(m + 1) * SUB], preferred_element_type=F32)
@@ -315,6 +329,8 @@
             for i, slot in enumerate(slots):
                 piece = both[i * TS:(i + 1) * TS].reshape(NY, 8, SUB).astype(BF16)
                 ybuf[slot, :, :, m * SUB:(m + 1) * SUB] = piece
+
+    def send(slots, part, parts, sem):
         for slot in slots:
             for k in [2, 1, 3]:
                 ry_copy(slot, part_cols(part, parts), sem, k).start()
@@ -346,13 +362,27 @@
         xt[m] = flip(inp[:, m * SUB:(m + 1) * SUB])
     first = [mine, slot_of_partner(0)]
     second = [slot_from(k) for k in near]
-    third = [slot_of_partner(k) for k in near]
-    fourth = [slot_from(far), slot_of_partner(far)]
+    def pick_slot(on_first, on_second):
+        return on_first + core * (on_second - on_first)
+
+    if near:
+        third = [
+            pick_slot(slot_from(far), slot_of_partner(near[0])),
+            pick_slot(slot_of_partner(near[0]), slot_of_partner(near[1])),
+        ]
+        fourth = [
+            pick_slot(slot_of_partner(near[1]), slot_of_partner(far)),
+            pick_slot(slot_of_partner(far), slot_from(far)),
+        ]
+    else:
+        third = []
+        fourth = [pick_slot(slot_from(far), slot_of_partner(far)), pick_slot(slot_of_partner(far), slot_from(far))]
     from_pair(0)
     spread_x(hga, ga_s, ga_r.at[far - 1], far).start()
     factors(first)
-    products(first, 0, 2, 0)
-    products(first, 1, 2, 0)
+    for part in range(2):
+        products(first, part, 2)
+        send(first, part, 2, 0)
     all_of(rta.at[pl.ds(0, NX - 1)], ra_r)
     for k in range(1, NX):
         spread_pair(rta, rp_s, rp_r, k).start()
@@ -361,20 +391,44 @@
     if near:
         factors(second)
         for part in range(2):
-            products(second, part, 2, 1)
+            products(second, part, 2)
+
+            @pl.when(core == 0)
+            def _():
+                send(second, part, 2, 1)
     for k in near:
         from_pair(k)
+    from_x(far)
     if near:
         factors(third)
-        products(third, 0, 2, 2)
-    from_x(far)
-    if near:
-        products(third, 1, 2, 2)
+        for part in range(2):
+            products(third, part, 2)
+            send(third, part, 2, 2)
+    @pl.when(core == 1)
+    def _():
+        pl.semaphore_wait(barrier, 2 * (NZ - 1) + 1)
+        tell(line_in, partner)
+
+    @pl.when(core == 0)
+    def _():
+        pl.semaphore_wait(line_in, 1)
+
     y_sums(first, 0, 1, 0)
     from_pair(far)
     factors(fourth)
     for part in range(2):
-        products(fourth, part, 2, 3 + part)
+        products(fourth, part, 2)
+        send(fourth, part, 2, 3 + part)
+    if near:
+        @pl.when(core == 1)
+        def _():
+            for part in range(2):
+                send(second, part, 2, 1)
+
+    if near:
+        @pl.when(core == 0)
+        def _():
+            y_sums(second, 0, 1, 1)
 
     all_of(rta.at[pl.ds(0, NX)], rp_r)
     whole = rta[...].reshape(T, F)
@@ -394,15 +448,17 @@
     up_sums = sums_over(uc, xt, ug, us, ul_out, NM)
     blocks = F // SUB
 
-    if near:
-        y_sums(second, 0, 1, 1)
-    down_sums(0, NM)
+    down_sums(0, 2 * NM // 3)
     if near:
         y_sums(third, 0, 1, 2)
-    gate_sums(0, blocks // 2)
+    down_sums(2 * NM // 3, NM)
     y_sums(fourth, 0, 2, 3)
-    gate_sums(blocks // 2, blocks)
     y_sums(fourth, 1, 2, 4)
+    if near:
+        @pl.when(core == 1)
+        def _():
+            y_sums(second, 0, 1, 1)
+    gate_sums(0, blocks)
     up_sums(0, blocks)
 
     total = zbuf[z].astype(F32)
@@ -464,7 +520,7 @@
         V((wid, TS, F), BF16), V((wid, TS, F), BF16),
         V((wid, NY, 8, D), BF16), V((wid, NY - 1, 8, D), BF16),
         V((NZ, 8, D), BF16), V((NZ - 1, 8, D), BF16),
-        dma(9), dma(NB),
+        pltpu.SemaphoreType.REGULAR, pltpu.SemaphoreType.REGULAR, dma(9), dma(NB),
         one, dma(NB), one, dma(NB), one, one, one, one,
         one, dma(NX - 1), one, dma(NX), one, one, one, one,
         one, dma(5), one, one,

time: 38.3 us -> 38 us (level)
  the two profiles are of different devices: /device:TPU:1 before, /device:TPU:33 now
where the time goes in v4:
time: 38 us
  Pallas kernels  37.3 us (98%)
  between operations  0.64 us (2%)
    pallas_call x1, Pallas kernels, shards(): pl.pallas_call(functools.partial(body, (NX, NY, NZ, T, D, F)), out_shape=...  36.6 us

profile of v4, /device:TPU:33, one launch (start us, length us, event | category | flops | bytes accessed | tf_op | source)
XLA Modules:
  0.0 38.0 jit_solution(10510372804880331112)
XLA Ops:
  0.6 36.6 %layer.1 = (bf16[8,1536]{1,0:T(8,128)(2,1)S(1)}, f32[12,1024]{1,0:T(8,128)S(1)}, f32[12,1024]{1,0:T(8,128)S(1)}, f32[8,1536]{1,0:T(8,128)S(1)}) custom-call(bf16[256,1536]{1,0:T(8,128)(2,1)} %inp_hbm.1, bf16[256,1024]{1,0:T(8,128)(2,1)} %gp_hbm.1, bf16[256,1024]{1,0:T(8,128)(2,1)} %up_hbm.1, bf16[256,1536]{1,0:T(8,128)(2,1)} %og_hbm.1, s32[768,1024]{1,0:T(8,128)} %gc_hbm.1, ...), custom_call_target="tpu_custom_call" | custom-call | tf_op jit(solution)/shard_map/layer/pallas_call | solution.py:528
  37.3 0.7 %hand_out.1 = (bf16[8,1536]{1,0:T(8,128)(2,1)}, f32[12,1024]{1,0:T(8,128)}, f32[12,1024]{1,0:T(8,128)}, f32[8,1536]{1,0:T(8,128)}) custom-call(bf16[8,1536]{1,0:T(8,128)(2,1)S(1)} %get-tuple-element.8.refs_0_, f32[12,1024]{1,0:T(8,128)S(1)} %get-tuple-element.9.refs_1_, f32[12,1024]{1,0:T(8,128)S(1)} %get-tuple-element.10.refs_2_, ...), custom_call_target="tpu_custom_call" | custom-call | tf_op jit(solution)/shard_map/hand_out/pallas_call | solution.py:541

commit v5 on v4

--- a/solution.py
+++ b/solution.py
@@ -297,7 +297,7 @@
     spread(hga, ga_s, lambda k: ga_r.at[k - 1], gp_s, lambda k: gp_r.at[k])
 
     def part_cols(part, parts):
-        return pl.ds(part * D // parts, D // parts)
+        return pl.ds(pl.multiple_of(part * (D // parts), SUB), D // parts)
 
     def ry_copy(slot, cols, sem, k):
         return remote(
@@ -321,14 +321,16 @@
             ug[rows, :] = (hg * act[rows, :]).astype(BF16)
 
     def products(slots, part, parts):
-        for m in range(part * NM // parts, (part + 1) * NM // parts):
+        for n in range(NM // parts):
+            m = part * (NM // parts) + n
+            cols = pl.ds(pl.multiple_of(m * SUB, SUB), SUB)
             left = jnp.concatenate([gg[slot_rows(slot), :] for slot in slots], axis=0)
-            both = jnp.dot(left, gwt[:, m * SUB:(m + 1) * SUB], preferred_element_type=F32)
+            both = jnp.dot(left, gwt[:, cols], preferred_element_type=F32)
             left = jnp.concatenate([ug[slot_rows(slot), :] for slot in slots], axis=0)
-            both = both + jnp.dot(left, uwt[:, m * SUB:(m + 1) * SUB], preferred_element_type=F32)
+            both = both + jnp.dot(left, uwt[:, cols], preferred_element_type=F32)
             for i, slot in enumerate(slots):
                 piece = both[i * TS:(i + 1) * TS].reshape(NY, 8, SUB).astype(BF16)
-                ybuf[slot, :, :, m * SUB:(m + 1) * SUB] = piece
+                ybuf[slot, :, :, cols] = piece
 
     def send(slots, part, parts, sem):
         for slot in slots:
@@ -380,7 +382,8 @@
     from_pair(0)
     spread_x(hga, ga_s, ga_r.at[far - 1], far).start()
     factors(first)
-    for part in range(2):
+    @pl.loop(0, 2)
+    def _(part):
         products(first, part, 2)
         send(first, part, 2, 0)
     all_of(rta.at[pl.ds(0, NX - 1)], ra_r)
@@ -390,7 +393,8 @@
         from_x(k)
     if near:
         factors(second)
-        for part in range(2):
+        @pl.loop(0, 2)
+        def _(part):
             products(second, part, 2)
 
             @pl.when(core == 0)
@@ -401,7 +405,8 @@
     from_x(far)
     if near:
         factors(third)
-        for part in range(2):
+        @pl.loop(0, 2)
+        def _(part):
             products(third, part, 2)
             send(third, part, 2, 2)
     @pl.when(core == 1)
@@ -416,7 +421,8 @@
     y_sums(first, 0, 1, 0)
     from_pair(far)
     factors(fourth)
-    for part in range(2):
+    @pl.loop(0, 2)
+    def _(part):
         products(fourth, part, 2)
         send(fourth, part, 2, 3 + part)
     if near:

time: 38 us -> 37.8 us (level)
  no operation moved by 1% of the time
where the time goes in v5:
time: 37.8 us
  Pallas kernels  37.1 us (98%)
  between operations  0.64 us (2%)
    pallas_call x1, Pallas kernels, shards(): pl.pallas_call(functools.partial(body, (NX, NY, NZ, T, D, F)), out_shape=...  36.4 us

profile of v5, /device:TPU:33, one launch (start us, length us, event | category | flops | bytes accessed | tf_op | source)
XLA Modules:
  0.0 37.8 jit_solution(2936221745895699052)
XLA Ops:
  0.6 36.4 %layer.1 = (bf16[8,1536]{1,0:T(8,128)(2,1)S(1)}, f32[12,1024]{1,0:T(8,128)S(1)}, f32[12,1024]{1,0:T(8,128)S(1)}, f32[8,1536]{1,0:T(8,128)S(1)}) custom-call(bf16[256,1536]{1,0:T(8,128)(2,1)} %inp_hbm.1, bf16[256,1024]{1,0:T(8,128)(2,1)} %gp_hbm.1, bf16[256,1024]{1,0:T(8,128)(2,1)} %up_hbm.1, bf16[256,1536]{1,0:T(8,128)(2,1)} %og_hbm.1, s32[768,1024]{1,0:T(8,128)} %gc_hbm.1, ...), custom_call_target="tpu_custom_call" | custom-call | tf_op jit(solution)/shard_map/layer/pallas_call | solution.py:534
  37.0 0.7 %hand_out.1 = (bf16[8,1536]{1,0:T(8,128)(2,1)}, f32[12,1024]{1,0:T(8,128)}, f32[12,1024]{1,0:T(8,128)}, f32[8,1536]{1,0:T(8,128)}) custom-call(bf16[8,1536]{1,0:T(8,128)(2,1)S(1)} %get-tuple-element.8.refs_0_, f32[12,1024]{1,0:T(8,128)S(1)} %get-tuple-element.9.refs_1_, f32[12,1024]{1,0:T(8,128)S(1)} %get-tuple-element.10.refs_2_, ...), custom_call_target="tpu_custom_call" | custom-call | tf_op jit(solution)/shard_map/hand_out/pallas_call | solution.py:547
